TPU v7x, 256 devices: a whole 4x4x8 slice. The times are simulated.
256 devices in a mesh: req: 32 (over z, x), mlp: 8 (over y, core).
Axes of the slice: x: 4, y: 4, z: 8, core: 2. Of those that a mesh axis runs over, the one named last changes fastest.
Arguments:
- tokens: bfloat16 [8192, 2048], P('req', 'mlp'), may hold values from -12 to 12
- segment_ids: int32 [8192], P('req'), may hold values from 0 to 16, never falling along the last dimension, each value on 1 to 4096 neighbouring positions
- page_source: int32 [512], P('req'), may hold values from 0 to 511, each once
- query_weight: bfloat16 [2048, 2048], P(None, 'mlp')
- key_weight: bfloat16 [2048, 2048], P(None, 'mlp')
- value_weight: bfloat16 [2048, 2048], P(None, 'mlp'), may hold values from -0.125 to 0.125
- out_weight: bfloat16 [2048, 2048], P('mlp')
- query_gain: float32 [2048], P('mlp'), may hold values from 0.5 to 9
- key_gain: float32 [2048], P('mlp'), may hold values from 0.5 to 9
- attention_gain: float32 [2048], P('mlp'), may hold values from 0.25 to 1.75
- gate_weight: bfloat16 [2048, 8192], P('req', 'mlp'), may hold values from -0.125 to 0.125
- up_weight: bfloat16 [2048, 8192], P('req', 'mlp'), may hold values from -0.125 to 0.125
- down_weight: bfloat16 [2048, 8192], P('req', 'mlp')
- feedforward_gain: float32 [2048], P('mlp'), may hold values from 0.25 to 1.75
Outputs:
- layer_out: bfloat16 [8192, 2048], P('req', 'mlp')
- page_cache: bfloat16 [512, 2, 16, 2048], P('req', None, None, 'mlp')
Inputs may be any that keep to these rules, and one draw needn't show every extreme that they name: `segment_ids`: segment ids never fall along the stream; each prompt has 1 to 4096 tokens and one has exactly 4096. `page_source`: each stream page appears once.
All inputs are finite; a program needn't handle non-finite values.
Results may differ from a plain program's by a relative error of at most 0.019.
The roundings to bfloat16 on the way count: a program that leaves them out, or rounds other values in their place, can miss the bound.
Values may be sent and summed in bfloat16 or wider, within the bound.
No kernel may reach another device: no remote copies, remote signals or barrier semaphores. Data moves between devices by JAX's collectives and lax.ppermute only.
A program may use at most 128 MiB of HBM per device.

v0:
```python
import jax
import jax.numpy as jnp
from jax import lax
from jax.sharding import PartitionSpec as P

HD = 128
PAGE = 16
rope_base = 500000.0
norm_eps = 1e-06


def rope_tables(positions, head_dim):
    half_dim = head_dim // 2
    inv_freq = rope_base ** (-(jnp.arange(half_dim, dtype=jnp.float32) * 2.0) / head_dim)
    angles = positions.astype(jnp.float32)[:, None] * inv_freq[None, :]
    return (jnp.cos(angles), jnp.sin(angles))


def rotate(values, cosine_table, sine_table, head_dim):
    tok_rows = values.shape[0]
    head_count = values.shape[1] // head_dim
    shaped = values.reshape(tok_rows, head_count, head_dim)
    half_dim = head_dim // 2
    first_half = shaped[..., :half_dim]
    second = shaped[..., half_dim:]
    cos_b = cosine_table[:, None, :]
    sin_b = sine_table[:, None, :]
    turned = jnp.concatenate(
        [first_half * cos_b - second * sin_b, second * cos_b + first_half * sin_b], axis=-1
    )
    return turned.reshape(tok_rows, head_count * head_dim)


def post_norm(branch_term, gain_vec, model_width):
    own_part = lax.psum_scatter(
        branch_term.astype(jnp.bfloat16), "mlp", scatter_dimension=1, tiled=True
    ).astype(jnp.float32)
    mean_square = lax.psum(jnp.sum(own_part * own_part, axis=1), "mlp") / model_width
    return own_part * lax.rsqrt(mean_square + norm_eps)[:, None] * gain_vec[None, :]


def per_device(
    tokens,
    segment_ids,
    page_source,
    query_weight,
    key_weight,
    value_weight,
    out_weight,
    query_gain,
    key_gain,
    attention_gain,
    gate_weight,
    up_weight,
    down_weight,
    feedforward_gain,
):
    tok_rows = tokens.shape[0]
    local_width = tokens.shape[1]
    model_width = query_weight.shape[0]
    head_dim = HD
    head_count = local_width // head_dim
    full_rows = lax.all_gather(tokens, "mlp", axis=1, tiled=True)
    query_proj = jnp.dot(full_rows, query_weight, preferred_element_type=jnp.float32)
    key_proj = jnp.dot(full_rows, key_weight, preferred_element_type=jnp.float32)
    value_proj = jnp.dot(full_rows, value_weight, preferred_element_type=jnp.float32)
    query_total, key_total = lax.psum(
        (jnp.sum(query_proj * query_proj, axis=1), jnp.sum(key_proj * key_proj, axis=1)), "mlp"
    )
    query_n = (
        query_proj * lax.rsqrt(query_total / model_width + norm_eps)[:, None] * query_gain[None, :]
    )
    key_n = key_proj * lax.rsqrt(key_total / model_width + norm_eps)[:, None] * key_gain[None, :]
    seg_total = lax.axis_size("req") // 2 + 1
    seg_range = jnp.arange(seg_total, dtype=jnp.int32)
    matches = segment_ids[:, None] == seg_range[None, :]
    counts = jnp.sum(matches.astype(jnp.int32), axis=0)
    totals = lax.psum(counts, "req")
    seg_starts = jnp.cumsum(totals) - totals
    row_base = lax.axis_index("req") * tok_rows
    global_index = row_base + jnp.arange(tok_rows, dtype=jnp.int32)
    own_start = jnp.sum(jnp.where(matches, seg_starts[None, :], 0), axis=1)
    positions = global_index - own_start
    cosine_table, sine_table = rope_tables(positions, head_dim)
    query_r = rotate(query_n, cosine_table, sine_table, head_dim).astype(jnp.bfloat16)
    key_r = rotate(key_n, cosine_table, sine_table, head_dim).astype(jnp.bfloat16)
    value_b = value_proj.astype(jnp.bfloat16)
    query_heads = query_r.reshape(tok_rows, head_count, head_dim)
    score_scale = head_dim ** (-0.5)
    pages_here = page_source.shape[0]
    page_offsets = jnp.arange(PAGE, dtype=jnp.int32)
    attn_init = (
        jnp.full((head_count, tok_rows), -1e30, jnp.float32),
        jnp.zeros((head_count, tok_rows), jnp.float32),
        jnp.zeros((tok_rows, head_count, head_dim), jnp.float32),
    )
    cache_init = jnp.zeros((pages_here, 2, PAGE, local_width), jnp.bfloat16)
    fold_state = attn_init + (cache_init,)
    fetched = (
        lax.all_gather(key_r, "req", axis=0, tiled=True),
        lax.all_gather(value_b, "req", axis=0, tiled=True),
        lax.all_gather(segment_ids, "req", axis=0, tiled=True),
    )
    key_part, value_part, seg_part = fetched
    row_count = key_part.shape[0]
    block_rows = 512

    def one_block(block_index, state):
        run_max, run_sum, run_out = state
        offset = block_index * block_rows
        key_block = lax.dynamic_slice_in_dim(key_part, offset, block_rows, 0).reshape(
            block_rows, head_count, head_dim
        )
        value_block = lax.dynamic_slice_in_dim(value_part, offset, block_rows, 0).reshape(
            block_rows, head_count, head_dim
        )
        seg_block = lax.dynamic_slice_in_dim(seg_part, offset, block_rows, 0)
        key_index = offset + jnp.arange(block_rows, dtype=jnp.int32)
        visible = (
            (segment_ids[:, None] == seg_block[None, :])
            & (global_index[:, None] >= key_index[None, :])
            & (key_index[None, :] >= 0)
        )
        scores = (
            jnp.einsum("thd,rhd->htr", query_heads, key_block, preferred_element_type=jnp.float32)
            * score_scale
        )
        masked = jnp.where(visible[None], scores, -1e30)
        new_max = jnp.maximum(run_max, jnp.max(masked, axis=2))
        weights = jnp.where(visible[None], jnp.exp(scores - new_max[:, :, None]), 0.0)
        factor = jnp.exp(run_max - new_max)
        run_sum = run_sum * factor + jnp.sum(weights, axis=2)
        update = jnp.einsum(
            "htr,rhd->thd",
            weights.astype(jnp.bfloat16),
            value_block,
            preferred_element_type=jnp.float32,
        )
        run_out = run_out * factor.T[:, :, None] + update
        return (new_max, run_sum, run_out)

    attn_state = lax.fori_loop(0, row_count // block_rows, one_block, fold_state[:3])
    place_key_part = fetched[0]
    row_count = place_key_part.shape[0]
    page_rows = page_source[:, None] * PAGE + page_offsets[None, :]
    in_piece = (page_rows >= 0) & (page_rows < row_count)
    clipped = jnp.clip(page_rows, 0, row_count - 1)
    stacked = jnp.stack([place_key_part[clipped], fetched[1][clipped]], axis=1)
    page_cache = jnp.where(in_piece[:, None, :, None], stacked, fold_state[3])
    run_max, run_sum, run_out, page_cache = (
        attn_state[0],
        attn_state[1],
        attn_state[2],
        page_cache,
    )
    attended = (run_out / run_sum.T[:, :, None]).reshape(tok_rows, local_width).astype(jnp.bfloat16)
    projected = jnp.dot(attended, out_weight, preferred_element_type=jnp.float32)
    residual = (
        tokens.astype(jnp.float32) + post_norm(projected, attention_gain, model_width)
    ).astype(jnp.bfloat16)
    normed = lax.all_gather(residual, "mlp", axis=1, tiled=True)
    contract = (((1,), (1,)), ((), ()))
    fetched = (
        lax.all_gather(gate_weight, "req", axis=0, tiled=True),
        lax.all_gather(up_weight, "req", axis=0, tiled=True),
    )
    gate_act = jnp.dot(normed, fetched[0], preferred_element_type=jnp.float32)
    up_act = jnp.dot(normed, fetched[1], preferred_element_type=jnp.float32)
    hidden = (jax.nn.silu(gate_act) * up_act).astype(jnp.bfloat16)
    down_act = lax.dot_general(
        hidden,
        lax.all_gather(down_weight, "req", axis=0, tiled=True),
        contract,
        preferred_element_type=jnp.float32,
    )
    layer_out = (
        residual.astype(jnp.float32) + post_norm(down_act, feedforward_gain, model_width)
    ).astype(jnp.bfloat16)
    return (layer_out, page_cache)


def solution(mesh):
    in_specs = (
        P("req", "mlp"),
        P("req"),
        P("req"),
        P(None, "mlp"),
        P(None, "mlp"),
        P(None, "mlp"),
        P("mlp", None),
        P("mlp"),
        P("mlp"),
        P("mlp"),
        P("req", "mlp"),
        P("req", "mlp"),
        P("req", "mlp"),
        P("mlp"),
    )
    out_specs = (P("req", "mlp"), P("req", None, None, "mlp"))
    return jax.shard_map(
        per_device, mesh=mesh, in_specs=in_specs, out_specs=out_specs, check_vma=False
    )
```

profile of v0, /device:TPU:1, one launch (start us, length us, event | category | flops | bytes accessed | tf_op | source)
XLA Modules:
  0.0 636.5 jit_solution(3490800853905953545)
XLA Ops:
  8.8 19.8 %psum.36 = s32[17]{0:T(128)S(1)} all-reduce(s32[17]{0:T(128)S(1)} %convert_reduce_fusion), channel_id=1, replica_groups=mesh['req'=32,'mlp'=8] {'req'}, use_global_device_ids=true, to_apply=%region_3.0 | all-reduce | flops 17 | bytes 136 | tf_op jit(solution)/shard_map/psum | solution.py:78
  29.7 1.2 multiply_cosine_fusion
  30.9 9.1 %all-gather.9.cloned.1.call-done = bf16[256,2048]{1,0:T(8,128)(2,1)} async-done(((bf16[256,256]{1,0:T(8,128)(2,1)}), bf16[256,2048]{1,0:T(8,128)(2,1)}) %all-gather.9.cloned.1.call-update) | async-done | bytes 1048592 | tf_op jit(solution)/shard_map/all_gather | solution.py:63
  40.0 2.1 multiply_reduce_fusion.1
  42.0 2.2 multiply_reduce_fusion
  44.2 12.1 %all-reduce = (f32[256]{0:T(256)S(1)}, f32[256]{0:T(256)S(1)}) all-reduce(f32[256]{0:T(256)S(1)} %get-tuple-element.290, f32[256]{0:T(256)S(1)} %get-tuple-element.292), channel_id=1, replica_groups=mesh['req'=32,'mlp'=8] {'mlp'}, use_global_device_ids=true, to_apply=%region_1.0 | all-reduce | flops 512 | bytes 4096 | tf_op jit(solution)/shard_map/psum | solution.py:67
  59.0 2.3 convolution_convert_fusion.2
  61.4 35.7 %all-gather = s32[32,1,256]{2,1,0:T(1,128)S(1)} all-gather(s32[1,1,256]{2,1,0:T(1,128)S(1)} %bitcast.69), channel_id=1, replica_groups=mesh['req'=32,'mlp'=8] {'req'}, dimensions={0}, use_global_device_ids=true | all-gather | bytes 33792 | tf_op jit(solution)/shard_map/all_gather | solution.py:102
  97.3 40.7 %all-gather.11.cloned.1.call-done = bf16[8192,256]{1,0:T(8,128)(2,1)} async-done(((bf16[256,256]{1,0:T(8,128)(2,1)}), bf16[8192,256]{1,0:T(8,128)(2,1)}) %all-gather.11.cloned.1.call-update) | async-done | bytes 4194320 | tf_op jit(solution)/shard_map/all_gather | solution.py:100
  138.0 81.7 %all-gather.13.cloned.1.call-done = bf16[8192,256]{1,0:T(8,128)(2,1)} async-done(((bf16[256,256]{1,0:T(8,128)(2,1)}), bf16[8192,256]{1,0:T(8,128)(2,1)}) %all-gather.13.cloned.1.call-update) | async-done | bytes 4194320 | tf_op jit(solution)/shard_map/all_gather | solution.py:101
  219.7 44.8 %while.18 = (s32[]{:T(128)}, f32[2,256]{1,0:T(2,128)S(1)}, f32[2,256]{1,0:T(2,128)S(1)}, f32[256,2,128]{0,2,1:T(8,128)S(1)}, s32[256]{0:T(256)S(1)}, /*index=5*/...) while((s32[]{:T(128)}, f32[2,256]{1,0:T(2,128)S(1)}, ...), condition=%wide.region_11.12_spmd.clone, body=%wide.region_8.11_spmd.clone.sunk | while | flops 137302784 | bytes 6994131 | solution.py:142
  220.1 1.1 constant_dynamic-slice_fusion.3
  222.9 1.1 constant_dynamic-slice_fusion.3
  225.7 1.1 constant_dynamic-slice_fusion.3
  228.5 1.1 constant_dynamic-slice_fusion.3
  231.3 1.1 constant_dynamic-slice_fusion.3
  234.1 1.1 constant_dynamic-slice_fusion.3
  264.6 1.5 convolution_convert_fusion.1
  266.8 32.4 %reduce-scatter.3.cloned.1.call-done = bf16[256,256]{1,0:T(8,128)(2,1)} async-done(((bf16[256,2048]{1,0:T(8,128)(2,1)}), bf16[256,256]{1,0:T(8,128)(2,1)}) %reduce-scatter.3.cloned.1.call-update) | async-done | bytes 131088 | tf_op jit(solution)/shard_map/reduce_scatter | solution.py:35
  300.2 14.8 %psum.38 = f32[256]{0:T(256)S(1)} all-reduce(f32[256]{0:T(256)S(1)} %fusion.16), channel_id=1, replica_groups=mesh['req'=32,'mlp'=8] {'mlp'}, use_global_device_ids=true, to_apply=%region_14.15 | all-reduce | flops 256 | bytes 2048 | tf_op jit(solution)/shard_map/psum | solution.py:38
  315.0 1.7 fusion.19
  318.2 62.7 %all-gather.17.cloned.1.call-done = bf16[2048,1024]{1,0:T(8,128)(2,1)} async-done(((bf16[64,1024]{1,0:T(8,128)(2,1)}), bf16[2048,1024]{1,0:T(8,128)(2,1)}) %all-gather.17.cloned.1.call-update) | async-done | bytes 4194320 | tf_op jit(solution)/shard_map/all_gather | solution.py:164
  380.9 28.9 %all-gather.15.cloned.1.call-done = bf16[256,2048]{1,0:T(8,128)(2,1)} async-done(((bf16[256,256]{1,0:T(8,128)(2,1)}), bf16[256,2048]{1,0:T(8,128)(2,1)}) %all-gather.15.cloned.1.call-update) | async-done | bytes 1048592 | tf_op jit(solution)/shard_map/all_gather | solution.py:161
  409.8 3.8 fusion.31
  413.6 77.5 %all-gather.19.cloned.1.call-done = bf16[2048,1024]{1,0:T(8,128)(2,1)} async-done(((bf16[64,1024]{1,0:T(8,128)(2,1)}), bf16[2048,1024]{1,0:T(8,128)(2,1)}) %all-gather.19.cloned.1.call-update) | async-done | bytes 4194320 | tf_op jit(solution)/shard_map/all_gather | solution.py:165
  491.1 81.2 %all-gather.21.cloned.1.call-done = bf16[2048,1024]{1,0:T(8,128)(2,1)} async-done(((bf16[64,1024]{1,0:T(8,128)(2,1)}), bf16[2048,1024]{1,0:T(8,128)(2,1)}) %all-gather.21.cloned.1.call-update) | async-done | bytes 4194320 | tf_op jit(solution)/shard_map/all_gather | solution.py:172
  572.3 7.1 %convolution_convert_fusion = bf16[256,2048]{1,0:T(8,128)(2,1)} fusion(bf16[2048,1024]{1,0:T(8,128)(2,1)} %all-gather.21.cloned.1.call-done, bf16[256,2048]{1,0:T(8,128)(2,1)S(1)} %copy-done.9, bf16[2048,1024]{1,0:T(8,128)(2,1)} %all-gather.19.cloned.1.call-done, f32[256,1024]{1,0:T(8,128)S(1)} %fusion.31), kind=kOutput, calls=%fused_computation.28 | convolution fusion | flops 2149580800 | bytes 11534336 | tf_op jit(solution)/shard_map/dot_general | solution.py:170
  579.7 3.7 gather_fusion
  583.4 3.7 gather_fusion.1
  587.9 24.6 %reduce-scatter.5.cloned.1.call-done = bf16[256,256]{1,0:T(8,128)(2,1)} async-done(((bf16[256,2048]{1,0:T(8,128)(2,1)}), bf16[256,256]{1,0:T(8,128)(2,1)}) %reduce-scatter.5.cloned.1.call-update) | async-done | bytes 131088 | tf_op jit(solution)/shard_map/reduce_scatter | solution.py:35
  613.5 14.7 %psum.39 = f32[256]{0:T(256)S(1)} all-reduce(f32[256]{0:T(256)S(1)} %fusion.20), channel_id=1, replica_groups=mesh['req'=32,'mlp'=8] {'mlp'}, use_global_device_ids=true, to_apply=%region_17.18 | all-reduce | flops 256 | bytes 2048 | tf_op jit(solution)/shard_map/psum | solution.py:38
  628.2 1.7 fusion.23
  (292 shorter events, 47.8 us)
Async XLA Ops:
  7.2 257.4 %copy-start = (bf16[256,2048]{1,0:T(8,128)(2,1)S(1)}, bf16[256,2048]{1,0:T(8,128)(2,1)}, u32[]{:S(2)}) copy-start(bf16[256,2048]{1,0:T(8,128)(2,1)} %param.22) | copy-start | bytes 3145732
  7.2 49.1 %copy-start.5 = (f32[256]{0:T(256)S(1)}, f32[256]{0:T(256)}, u32[]{:S(2)}) copy-start(f32[256]{0:T(256)} %param.24) | copy-start | bytes 3076
  7.2 49.5 %copy-start.6 = (f32[256]{0:T(256)S(1)}, f32[256]{0:T(256)}, u32[]{:S(2)}) copy-start(f32[256]{0:T(256)} %param.23) | copy-start | bytes 3076
  7.2 32.8 %all-gather.9.cloned.1.call-start = ((), (), s32[]{:S(2)}) async-start(), calls=%async_computation.2 | async-start | bytes 1179648 | tf_op jit(solution)/shard_map/all_gather | solution.py:63
  7.9 130.0 %all-gather.11.cloned.1.call-start = ((), (), s32[]{:S(2)}) async-start(), calls=%async_computation.3 | async-start | bytes 4325376 | tf_op jit(solution)/shard_map/all_gather | solution.py:100
  42.0 17.0 %copy-start.1 = (bf16[256,2048]{1,0:T(8,128)(2,1)S(1)}, bf16[256,2048]{1,0:T(8,128)(2,1)}, u32[]{:S(2)}) copy-start(bf16[256,2048]{1,0:T(8,128)(2,1)} %all-gather.9.cloned.1.call-done) | copy-start | bytes 3145732
  56.3 5.1 copy-start.4
  58.9 160.8 %all-gather.13.cloned.1.call-start = ((), (), s32[]{:S(2)}) async-start(), calls=%async_computation.4 | async-start | bytes 4325376 | tf_op jit(solution)/shard_map/all_gather | solution.py:101
  61.3 237.8 %reduce-scatter.3.cloned.1.call-start = ((), (), s32[]{:S(2)}) async-start(), calls=%async_computation.5 | async-start | bytes 1179648 | tf_op jit(solution)/shard_map/reduce_scatter | solution.py:35
  219.7 95.2 %copy-start.3 = (bf16[256,256]{1,0:T(8,128)(2,1)S(1)}, bf16[256,256]{1,0:T(8,128)(2,1)}, u32[]{:S(2)}) copy-start(bf16[256,256]{1,0:T(8,128)(2,1)} %param.16) | copy-start | bytes 393220
  219.7 95.2 %copy-start.7 = (f32[256]{0:T(256)S(1)}, f32[256]{0:T(256)}, u32[]{:S(2)}) copy-start(f32[256]{0:T(256)} %param.25) | copy-start | bytes 3076
  266.1 114.8 %all-gather.17.cloned.1.call-start = ((), (), s32[]{:S(2)}) async-start(), calls=%async_computation.7 | async-start | bytes 4325376 | tf_op jit(solution)/shard_map/all_gather | solution.py:164
  266.7 143.0 %all-gather.15.cloned.1.call-start = ((), (), s32[]{:S(2)}) async-start(), calls=%async_computation.6 | async-start | bytes 1179648 | tf_op jit(solution)/shard_map/all_gather | solution.py:161
  316.7 174.5 %all-gather.19.cloned.1.call-start = ((), (), s32[]{:S(2)}) async-start(), calls=%async_computation.8 | async-start | bytes 4325376 | tf_op jit(solution)/shard_map/all_gather | solution.py:165
  317.4 254.9 %all-gather.21.cloned.1.call-start = ((), (), s32[]{:S(2)}) async-start(), calls=%async_computation.9 | async-start | bytes 4325376 | tf_op jit(solution)/shard_map/all_gather | solution.py:172
  318.2 294.3 %reduce-scatter.5.cloned.1.call-start = ((), (), s32[]{:S(2)}) async-start(), calls=%async_computation.10 | async-start | bytes 1179648 | tf_op jit(solution)/shard_map/reduce_scatter | solution.py:35
  409.8 162.5 %copy-start.9 = (bf16[256,2048]{1,0:T(8,128)(2,1)S(1)}, bf16[256,2048]{1,0:T(8,128)(2,1)}, u32[]{:S(2)}) copy-start(bf16[256,2048]{1,0:T(8,128)(2,1)} %all-gather.15.cloned.1.call-done) | copy-start | bytes 3145732
  413.6 165.8 %copy-start.10 = (s32[16]{0:T(128)S(1)}, s32[16]{0:T(128)}, u32[]{:S(2)}) copy-start(s32[16]{0:T(128)} %param.18) | copy-start | bytes 196
  413.6 214.6 %copy-start.8 = (f32[256]{0:T(256)S(1)}, f32[256]{0:T(256)}, u32[]{:S(2)}) copy-start(f32[256]{0:T(256)} %param.29) | copy-start | bytes 3076
  579.4 48.8 %copy-start.2 = (bf16[256,256]{1,0:T(8,128)(2,1)S(1)}, bf16[256,256]{1,0:T(8,128)(2,1)}, u32[]{:S(2)}) copy-start(bf16[256,256]{1,0:T(8,128)(2,1)} %fusion.19) | copy-start | bytes 393220
Sparse Core Ops, SparseCore 0:
  9.8 30.0 all-gather.8
  59.1 78.8 all-gather.10
  141.1 78.5 all-gather.12
  266.3 32.8 reduce-scatter.2
  301.6 79.2 all-gather.16
  383.2 26.5 all-gather.14
  412.3 78.7 all-gather.18
  493.7 78.5 all-gather.20
  579.5 32.8 reduce-scatter.4
where the time goes:
time: 637 us; the launch traced here: 636 us
  waiting for transfers between devices  441 us (69%)
  blocking collectives  97.1 us (15%)
  local copies, waits for them, and re-layouts  31.1 us (5%)
  matrix products  31 us (5%)
  other arithmetic  20.1 us (3%)
  between operations  14.1 us (2%)
    all_gather x1, waiting for transfers between devices, per_device(): lax.all_gather(value_b, 'req', axis=0, tiled=True)  81.7 us
    all_gather x1, waiting for transfers between devices, per_device(): lax.all_gather(down_weight, 'req', axis=0, tiled=True)  81.2 us
    all_gather x1, waiting for transfers between devices, per_device(): lax.all_gather(up_weight, 'req', axis=0, tiled=True)  77.5 us
    all_gather x1, waiting for transfers between devices, per_device(): lax.all_gather(gate_weight, 'req', axis=0, tiled=True)  62.7 us
    reduce_scatter x2, waiting for transfers between devices, post_norm(): lax.psum_scatter(branch_term.astype(jnp.bfloat16), 'mlp', scatter_dimensi...  57 us
    all_gather x1, waiting for transfers between devices, per_device(): lax.all_gather(key_r, 'req', axis=0, tiled=True)  40.7 us
    all_gather x1, blocking collectives, per_device(): lax.all_gather(segment_ids, 'req', axis=0, tiled=True)  35.7 us
    psum x2, blocking collectives, post_norm(): lax.psum(jnp.sum(own_part * own_part, axis=1), 'mlp') / model_width  29.5 us
  transfers between devices with their start and end apart: 9, of which 9 were waited for; matrix products, arithmetic and copies ran while one was open for 3% of the time, Pallas kernels for 0%

commit v1 on v0

--- a/solution.py
+++ b/solution.py
@@ -158,7 +158,24 @@
     residual = (
         tokens.astype(jnp.float32) + post_norm(projected, attention_gain, model_width)
     ).astype(jnp.bfloat16)
-    normed = lax.all_gather(residual, "mlp", axis=1, tiled=True)
+    size, mine, rows = (lax.axis_size("mlp"), lax.axis_index("mlp"), residual.shape[1])
+    ahead = [(i, (i + 1) % size) for i in range(size)]
+    downward = [(i, (i - 1) % size) for i in range(size)]
+    result = jnp.zeros((*residual.shape[:1], size * rows, *residual.shape[1 + 1 :]), residual.dtype)
+    result = lax.dynamic_update_slice_in_dim(result, residual, mine * rows, axis=1)
+    from_left = from_right = residual
+    halfway = size // 2
+    for step in range(1, halfway + 1):
+        from_left = lax.ppermute(from_left, "mlp", ahead)
+        result = lax.dynamic_update_slice_in_dim(
+            result, from_left, (mine - step) % size * rows, axis=1
+        )
+        if step < size - halfway:
+            from_right = lax.ppermute(from_right, "mlp", downward)
+            result = lax.dynamic_update_slice_in_dim(
+                result, from_right, (mine + step) % size * rows, axis=1
+            )
+    normed = result
     contract = (((1,), (1,)), ((), ()))
     fetched = (
         lax.all_gather(gate_weight, "req", axis=0, tiled=True),

time: 637 us -> 608 us (0.954)
  waiting for transfers between devices: 441 us -> 403 us
  starting transfers between devices: 0.36 us -> 10.2 us
    all_gather x1 -> x0, waiting for transfers between devices: 28.9 us -> none  [per_device(): normed = lax.all_gather(residual, 'mlp', axis=1, tiled=True)]
    all_gather x1, waiting for transfers between devices: 62.7 us -> 45.7 us  [per_device(): lax.all_gather(gate_weight, 'req', axis=0, tiled=True)]
    ppermute x0 -> x7, starting transfers between devices: none -> 9.86 us  [the longest x3 6.69 us: per_device(): from_right = lax.ppermute(from_right, 'mlp', downward)]
    ppermute x0 -> x7, waiting for transfers between devices: none -> 9.05 us  [the longest x4 7.57 us: per_device(): from_left = lax.ppermute(from_left, 'mlp', ahead)]
  transfers between devices with their start and end apart: 9 -> 15, of which waited for: 9 -> 15; matrix products, arithmetic and copies ran while one was open for 3% -> 3% of each run, Pallas kernels for 0% -> 0%
where the time goes in v1:
time: 608 us; the launch traced here: 607 us
  waiting for transfers between devices  403 us (66%)
  blocking collectives  97.3 us (16%)
  local copies, waits for them, and re-layouts  31.3 us (5%)
  matrix products  30.4 us (5%)
  other arithmetic  19.4 us (3%)
  between operations  14.5 us (2%)
  starting transfers between devices  10.2 us (2%)
    all_gather x1, waiting for transfers between devices, per_device(): lax.all_gather(value_b, 'req', axis=0, tiled=True)  81.7 us
    all_gather x1, waiting for transfers between devices, per_device(): lax.all_gather(down_weight, 'req', axis=0, tiled=True)  81.2 us
    all_gather x1, waiting for transfers between devices, per_device(): lax.all_gather(up_weight, 'req', axis=0, tiled=True)  77.5 us
    reduce_scatter x2, waiting for transfers between devices, post_norm(): lax.psum_scatter(branch_term.astype(jnp.bfloat16), 'mlp', scatter_dimensi...  55.5 us
    all_gather x1, waiting for transfers between devices, per_device(): lax.all_gather(gate_weight, 'req', axis=0, tiled=True)  45.7 us
    all_gather x1, waiting for transfers between devices, per_device(): lax.all_gather(key_r, 'req', axis=0, tiled=True)  40.7 us
    all_gather x1, blocking collectives, per_device(): lax.all_gather(segment_ids, 'req', axis=0, tiled=True)  35.7 us
    psum x2, blocking collectives, post_norm(): lax.psum(jnp.sum(own_part * own_part, axis=1), 'mlp') / model_width  29.7 us
  transfers between devices with their start and end apart: 15, of which 15 were waited for; matrix products, arithmetic and copies ran while one was open for 3% of the time, Pallas kernels for 0%

profile of v1, /device:TPU:1, one launch (start us, length us, event | category | flops | bytes accessed | tf_op | source)
XLA Modules:
  0.0 607.4 jit_solution(18120549850336110858)
XLA Ops:
  8.8 19.8 %psum.36 = s32[17]{0:T(128)S(1)} all-reduce(s32[17]{0:T(128)S(1)} %convert_reduce_fusion), channel_id=1, replica_groups=mesh['req'=32,'mlp'=8] {'req'}, use_global_device_ids=true, to_apply=%region_3.0 | all-reduce | flops 17 | bytes 136 | tf_op jit(solution)/shard_map/psum | solution.py:78
  29.7 1.2 multiply_cosine_fusion
  30.9 9.1 %all-gather.8.cloned.1.call-done = bf16[256,2048]{1,0:T(8,128)(2,1)} async-done(((bf16[256,256]{1,0:T(8,128)(2,1)}), bf16[256,2048]{1,0:T(8,128)(2,1)}) %all-gather.8.cloned.1.call-update) | async-done | bytes 1048592 | tf_op jit(solution)/shard_map/all_gather | solution.py:63
  40.0 2.1 multiply_reduce_fusion.1
  42.0 2.2 multiply_reduce_fusion
  44.2 12.1 %all-reduce = (f32[256]{0:T(256)S(1)}, f32[256]{0:T(256)S(1)}) all-reduce(f32[256]{0:T(256)S(1)} %get-tuple-element.292, f32[256]{0:T(256)S(1)} %get-tuple-element.294), channel_id=1, replica_groups=mesh['req'=32,'mlp'=8] {'mlp'}, use_global_device_ids=true, to_apply=%region_1.0 | all-reduce | flops 512 | bytes 4096 | tf_op jit(solution)/shard_map/psum | solution.py:67
  59.0 2.3 convolution_convert_fusion.2
  61.4 35.7 %all-gather = s32[32,1,256]{2,1,0:T(1,128)S(1)} all-gather(s32[1,1,256]{2,1,0:T(1,128)S(1)} %bitcast.69), channel_id=1, replica_groups=mesh['req'=32,'mlp'=8] {'req'}, dimensions={0}, use_global_device_ids=true | all-gather | bytes 33792 | tf_op jit(solution)/shard_map/all_gather | solution.py:102
  97.3 40.7 %all-gather.10.cloned.1.call-done = bf16[8192,256]{1,0:T(8,128)(2,1)} async-done(((bf16[256,256]{1,0:T(8,128)(2,1)}), bf16[8192,256]{1,0:T(8,128)(2,1)}) %all-gather.10.cloned.1.call-update) | async-done | bytes 4194320 | tf_op jit(solution)/shard_map/all_gather | solution.py:100
  138.0 81.7 %all-gather.12.cloned.1.call-done = bf16[8192,256]{1,0:T(8,128)(2,1)} async-done(((bf16[256,256]{1,0:T(8,128)(2,1)}), bf16[8192,256]{1,0:T(8,128)(2,1)}) %all-gather.12.cloned.1.call-update) | async-done | bytes 4194320 | tf_op jit(solution)/shard_map/all_gather | solution.py:101
  219.7 44.8 %while.18 = (s32[]{:T(128)}, f32[2,256]{1,0:T(2,128)S(1)}, f32[2,256]{1,0:T(2,128)S(1)}, f32[256,2,128]{0,2,1:T(8,128)S(1)}, s32[256]{0:T(256)S(1)}, /*index=5*/...) while((s32[]{:T(128)}, f32[2,256]{1,0:T(2,128)S(1)}, ...), condition=%wide.region_11.12_spmd.clone, body=%wide.region_8.11_spmd.clone.sunk | while | flops 137302784 | bytes 6994131 | solution.py:142
  220.1 1.1 constant_dynamic-slice_fusion.3
  222.9 1.1 constant_dynamic-slice_fusion.3
  225.7 1.1 constant_dynamic-slice_fusion.3
  264.6 1.4 convolution_convert_fusion.1
  268.1 31.0 %reduce-scatter.3.cloned.1.call-done = bf16[256,256]{1,0:T(8,128)(2,1)} async-done(((bf16[256,2048]{1,0:T(8,128)(2,1)}), bf16[256,256]{1,0:T(8,128)(2,1)}) %reduce-scatter.3.cloned.1.call-update) | async-done | bytes 131088 | tf_op jit(solution)/shard_map/reduce_scatter | solution.py:35
  300.1 14.9 %psum.38 = f32[256]{0:T(256)S(1)} all-reduce(f32[256]{0:T(256)S(1)} %fusion.15), channel_id=1, replica_groups=mesh['req'=32,'mlp'=8] {'mlp'}, use_global_device_ids=true, to_apply=%region_14.15 | all-reduce | flops 256 | bytes 2048 | tf_op jit(solution)/shard_map/psum | solution.py:38
  316.2 1.4 collective-permute-start.1
  318.4 2.2 collective-permute-start.2
  321.0 2.2 collective-permute-start.3
  325.7 3.1 collective-permute-start.5
  330.1 5.2 collective-permute-done.6
  335.2 45.7 %all-gather.14.cloned.1.call-done = bf16[2048,1024]{1,0:T(8,128)(2,1)} async-done(((bf16[64,1024]{1,0:T(8,128)(2,1)}), bf16[2048,1024]{1,0:T(8,128)(2,1)}) %all-gather.14.cloned.1.call-update) | async-done | bytes 4194320 | tf_op jit(solution)/shard_map/all_gather | solution.py:181
  380.9 3.4 fusion.33
  384.4 77.5 %all-gather.16.cloned.1.call-done = bf16[2048,1024]{1,0:T(8,128)(2,1)} async-done(((bf16[64,1024]{1,0:T(8,128)(2,1)}), bf16[2048,1024]{1,0:T(8,128)(2,1)}) %all-gather.16.cloned.1.call-update) | async-done | bytes 4194320 | tf_op jit(solution)/shard_map/all_gather | solution.py:182
  462.0 81.2 %all-gather.18.cloned.1.call-done = bf16[2048,1024]{1,0:T(8,128)(2,1)} async-done(((bf16[64,1024]{1,0:T(8,128)(2,1)}), bf16[2048,1024]{1,0:T(8,128)(2,1)}) %all-gather.18.cloned.1.call-update) | async-done | bytes 4194320 | tf_op jit(solution)/shard_map/all_gather | solution.py:189
  543.1 7.0 %convolution_convert_fusion = bf16[256,2048]{1,0:T(8,128)(2,1)} fusion(bf16[2048,1024]{1,0:T(8,128)(2,1)} %all-gather.18.cloned.1.call-done, f32[256,1024]{1,0:T(8,128)S(1)} %fusion.33, bf16[256,2048]{1,0:T(8,128)(2,1)S(1)} %constant_dynamic-update-slice_fusion, bf16[2048,1024]{1,0:T(8,128)(2,1)} %all-gather.16.cloned.1.call-done), kind=kOutput, calls=%fused_computation.28 | convolution fusion | flops 2149580800 | bytes 11534336 | tf_op jit(solution)/shard_map/dot_general | solution.py:187
  550.4 3.7 gather_fusion
  554.1 3.7 gather_fusion.1
  558.6 24.5 %reduce-scatter.5.cloned.1.call-done = bf16[256,256]{1,0:T(8,128)(2,1)} async-done(((bf16[256,2048]{1,0:T(8,128)(2,1)}), bf16[256,256]{1,0:T(8,128)(2,1)}) %reduce-scatter.5.cloned.1.call-update) | async-done | bytes 131088 | tf_op jit(solution)/shard_map/reduce_scatter | solution.py:35
  584.1 14.8 %psum.39 = f32[256]{0:T(256)S(1)} all-reduce(f32[256]{0:T(256)S(1)} %fusion.19), channel_id=1, replica_groups=mesh['req'=32,'mlp'=8] {'mlp'}, use_global_device_ids=true, to_apply=%region_17.18 | all-reduce | flops 256 | bytes 2048 | tf_op jit(solution)/shard_map/psum | solution.py:38
  598.9 1.7 fusion.22
  (307 shorter events, 56.9 us)
Async XLA Ops:
  7.2 257.5 %copy-start = (bf16[256,2048]{1,0:T(8,128)(2,1)S(1)}, bf16[256,2048]{1,0:T(8,128)(2,1)}, u32[]{:S(2)}) copy-start(bf16[256,2048]{1,0:T(8,128)(2,1)} %param.22) | copy-start | bytes 3145732
  7.2 49.1 %copy-start.4 = (f32[256]{0:T(256)S(1)}, f32[256]{0:T(256)}, u32[]{:S(2)}) copy-start(f32[256]{0:T(256)} %param.24) | copy-start | bytes 3076
  7.2 49.5 %copy-start.5 = (f32[256]{0:T(256)S(1)}, f32[256]{0:T(256)}, u32[]{:S(2)}) copy-start(f32[256]{0:T(256)} %param.23) | copy-start | bytes 3076
  7.2 32.8 %all-gather.8.cloned.1.call-start = ((), (), s32[]{:S(2)}) async-start(), calls=%async_computation.2 | async-start | bytes 1179648 | tf_op jit(solution)/shard_map/all_gather | solution.py:63
  7.9 130.0 %all-gather.10.cloned.1.call-start = ((), (), s32[]{:S(2)}) async-start(), calls=%async_computation.3 | async-start | bytes 4325376 | tf_op jit(solution)/shard_map/all_gather | solution.py:100
  42.0 17.0 %copy-start.1 = (bf16[256,2048]{1,0:T(8,128)(2,1)S(1)}, bf16[256,2048]{1,0:T(8,128)(2,1)}, u32[]{:S(2)}) copy-start(bf16[256,2048]{1,0:T(8,128)(2,1)} %all-gather.8.cloned.1.call-done) | copy-start | bytes 3145732
  56.3 5.1 copy-start.3
  58.9 160.8 %all-gather.12.cloned.1.call-start = ((), (), s32[]{:S(2)}) async-start(), calls=%async_computation.4 | async-start | bytes 4325376 | tf_op jit(solution)/shard_map/all_gather | solution.py:101
  61.4 237.7 %reduce-scatter.3.cloned.1.call-start = ((), (), s32[]{:S(2)}) async-start(), calls=%async_computation.5 | async-start | bytes 1179648 | tf_op jit(solution)/shard_map/reduce_scatter | solution.py:35
  264.6 50.6 %copy-start.2 = (bf16[256,256]{1,0:T(8,128)(2,1)S(1)}, bf16[256,256]{1,0:T(8,128)(2,1)}, u32[]{:S(2)}) copy-start(bf16[256,256]{1,0:T(8,128)(2,1)} %param.16) | copy-start | bytes 393220
  264.6 50.6 %copy-start.6 = (f32[256]{0:T(256)S(1)}, f32[256]{0:T(256)}, u32[]{:S(2)}) copy-start(f32[256]{0:T(256)} %param.25) | copy-start | bytes 3076
  266.1 114.8 %all-gather.14.cloned.1.call-start = ((), (), s32[]{:S(2)}) async-start(), calls=%async_computation.6 | async-start | bytes 4325376 | tf_op jit(solution)/shard_map/all_gather | solution.py:181
  266.7 195.3 %all-gather.16.cloned.1.call-start = ((), (), s32[]{:S(2)}) async-start(), calls=%async_computation.7 | async-start | bytes 4325376 | tf_op jit(solution)/shard_map/all_gather | solution.py:182
  267.3 275.8 %all-gather.18.cloned.1.call-start = ((), (), s32[]{:S(2)}) async-start(), calls=%async_computation.8 | async-start | bytes 4325376 | tf_op jit(solution)/shard_map/all_gather | solution.py:189
  268.0 315.1 %reduce-scatter.5.cloned.1.call-start = ((), (), s32[]{:S(2)}) async-start(), calls=%async_computation.9 | async-start | bytes 1179648 | tf_op jit(solution)/shard_map/reduce_scatter | solution.py:35
  316.2 2.2 collective-permute-start
  316.2 4.8 collective-permute-start.1
  318.4 5.6 collective-permute-start.2
  321.0 4.6 collective-permute-start.3
  324.0 5.6 collective-permute-start.4
  325.7 4.4 collective-permute-start.5
  329.6 5.6 collective-permute-start.6
  384.4 165.7 %copy-start.8 = (s32[16]{0:T(128)S(1)}, s32[16]{0:T(128)}, u32[]{:S(2)}) copy-start(s32[16]{0:T(128)} %param.18) | copy-start | bytes 196
  384.4 214.5 %copy-start.7 = (f32[256]{0:T(256)S(1)}, f32[256]{0:T(256)}, u32[]{:S(2)}) copy-start(f32[256]{0:T(256)} %param.29) | copy-start | bytes 3076
Sparse Core Ops, SparseCore 0:
  9.8 30.0 all-gather.7
  59.1 78.8 all-gather.9
  141.1 78.5 all-gather.11
  266.2 32.7 reduce-scatter.2
  301.5 79.4 all-gather.13
  383.4 78.5 all-gather.15
  464.5 78.5 all-gather.17
  550.2 32.8 reduce-scatter.4
